TPU v7x, 128 devices: a whole 4x4x4 slice. The times are simulated.
128 devices in a mesh: req: 8 (over y, core), row: 4 (over z), col: 4 (over x).
Axes of the slice: x: 4, y: 4, z: 4, core: 2. Of those that a mesh axis runs over, the one named last changes fastest.
Arguments:
- tokens: bfloat16 [16384, 1024], P(('req', 'row')), may hold values from -6 to 6
- norm_gain: float32 [1024], replicated, may hold values from 0.5 to 1.5
- w_attn: bfloat16 [5, 1024, 1024], P(None, 'row', 'col'), may hold values from -1 to 1
- persist_kv: bfloat16 [2, 16, 1024], P(None, None, 'col'), may hold values from -6 to 6
- kv_pool: bfloat16 [32, 32, 1, 256, 2, 1024], P(('req', 'row'), None, None, None, None, 'col'), may hold values from -6 to 6
- cache_len: int32 [32], replicated, may hold values from 0 to 8192, as said below
- mem_state: float32 [32, 8, 128, 128], P(('req', 'row'), 'col'), may hold values from -0.5 to 0.5
- decay: float32 [32, 8, 8], P(('req', 'row'), None, 'col'), may hold values from 0.6 to 1
- rate: float32 [32, 8, 8], P(('req', 'row'), None, 'col'), may hold values from 0.05 to 0.5
Outputs:
- mixed: bfloat16 [16384, 1024], P(('req', 'row'), 'col')
- new_state: float32 [32, 8, 128, 128], P(('req', 'row'), 'col')
Inputs may be any that keep to these rules, and one draw needn't show every extreme that they name: `cache_len`: cached tokens before each block; some block has exactly 8192.
All inputs are finite; a program needn't handle non-finite values.
Results may differ from a plain program's by a relative error of at most 0.006.
Values may be sent and summed in bfloat16 or wider, within the bound.
A program may use at most 192 MiB of HBM per device.

v0:
```python
import jax
import jax.numpy as jnp
from jax import lax
from jax.sharding import PartitionSpec as P

HD = 128
NP = 16
SEG = 64


negative_fill = -1e30


def attend(query_heads, key_heads, value_heads, allowed):
    scores = jnp.einsum(
        "...shd,...khd->...hsk", query_heads, key_heads, preferred_element_type=jnp.float32
    ) * query_heads.shape[-1] ** (-0.5)
    allowed = allowed[..., None, :, :]
    scores = jnp.where(allowed, scores, negative_fill)
    maxima = jnp.max(scores, axis=-1)
    probabilities = jnp.where(allowed, jnp.exp(scores - maxima[..., None]), 0.0)
    totals = jnp.sum(probabilities, axis=-1)
    weighted = jnp.einsum(
        "...hsk,...khd->...shd",
        probabilities.astype(jnp.bfloat16),
        value_heads,
        preferred_element_type=jnp.float32,
    )
    return (weighted, jnp.swapaxes(maxima, -1, -2), jnp.swapaxes(totals, -1, -2))


def combine_parts(first_part, second_part):
    output_a, maxima_a, totals_a = first_part
    output_b, maxima_b, totals_b = second_part
    highest = jnp.maximum(maxima_a, maxima_b)
    factor_a = jnp.exp(maxima_a - highest)
    factor_b = jnp.exp(maxima_b - highest)
    merged = output_a * factor_a[..., None] + output_b * factor_b[..., None]
    return (merged, highest, totals_a * factor_a + totals_b * factor_b)


def shards(tokens, norm_gain, w_attn, persist_kv, kv_pool, cache_len, mem_state, decay, rate):
    pool_size = lax.axis_size(("req", "row"))
    my_index = lax.axis_index(("req", "row"))
    column = lax.axis_index("col")
    length = tokens.shape[0]
    local_width = w_attn.shape[2]
    heads_here = local_width // HD
    xfloat = tokens.astype(jnp.float32)
    normed = (
        xfloat * lax.rsqrt(jnp.mean(xfloat * xfloat, axis=-1, keepdims=True) + 1e-05) * norm_gain
    ).astype(jnp.bfloat16)
    gathered = lax.all_gather(w_attn, "row", axis=1, tiled=True)
    projected = jnp.einsum("sd,wdc->wsc", normed, gathered[:4], preferred_element_type=jnp.float32)
    queries = projected[0].astype(jnp.bfloat16).reshape(length, heads_here, HD)
    keys_own = projected[1].astype(jnp.bfloat16).reshape(length, heads_here, HD)
    values_own = projected[2].astype(jnp.bfloat16).reshape(length, heads_here, HD)
    gate_open = jax.nn.sigmoid(projected[3]).reshape(length, heads_here, HD)
    persist = persist_kv.reshape(2, NP, heads_here, HD)
    keys_cat = jnp.concatenate([persist[0], keys_own], axis=0)
    vals_cat = jnp.concatenate([persist[1], values_own], axis=0)
    positions = jnp.arange(length, dtype=jnp.int32)
    causal = positions[:, None] >= positions[None, :]
    allowed = jnp.concatenate([jnp.ones((length, NP), dtype=bool), causal], axis=1)
    local_part = attend(queries, keys_cat, vals_cat, allowed)
    page_pool = kv_pool[0]
    slot_count = page_pool.shape[1]
    page_len = page_pool.shape[2]
    slot_ids = jnp.arange(slot_count, dtype=jnp.int32)[None, :, None]
    offsets = jnp.arange(page_len, dtype=jnp.int32)[None, None, :]
    peer_ids = jnp.arange(pool_size, dtype=jnp.int32)[:, None, None]
    everyone = lax.all_gather(queries[None], ("req", "row"), axis=0, tiled=True)
    page_ids = slot_ids * pool_size + (my_index - peer_ids) % pool_size
    places = (page_ids * page_len + offsets).reshape(pool_size, slot_count * page_len)
    usable = (places < cache_len[:, None])[:, None, :]
    cache_keys = page_pool[:, :, :, 0].reshape(pool_size, slot_count * page_len, heads_here, HD)
    cache_vals = page_pool[:, :, :, 1].reshape(pool_size, slot_count * page_len, heads_here, HD)
    part_out, part_max, part_tot = attend(everyone, cache_keys, cache_vals, usable)
    got_out, got_max, got_tot = (
        lax.all_to_all(part_out, ("req", "row"), split_axis=0, concat_axis=0, tiled=True),
        lax.all_to_all(part_max, ("req", "row"), split_axis=0, concat_axis=0, tiled=True),
        lax.all_to_all(part_tot, ("req", "row"), split_axis=0, concat_axis=0, tiled=True),
    )
    highest = jnp.max(got_max, axis=0)
    scaling = jnp.exp(got_max - highest[None])
    cache_part = (
        jnp.sum(got_out * scaling[..., None], axis=0),
        highest,
        jnp.sum(got_tot * scaling, axis=0),
    )
    total_part = combine_parts(local_part, cache_part)
    attended = total_part[0] / total_part[2][..., None]
    query_float = queries.astype(jnp.float32)
    key_float = keys_own.astype(jnp.float32)
    value_float = values_own.astype(jnp.float32)
    query_unit = query_float * lax.rsqrt(
        jnp.sum(query_float * query_float, axis=-1, keepdims=True) + 1e-06
    )
    key_unit = key_float * lax.rsqrt(jnp.sum(key_float * key_float, axis=-1, keepdims=True) + 1e-06)
    memory = mem_state[0]
    outputs = []
    for segment in range(length // SEG):
        lower = segment * SEG
        seg_query = query_unit[lower : lower + SEG]
        seg_keys = key_unit[lower : lower + SEG]
        seg_values = value_float[lower : lower + SEG]
        outputs.append(
            jnp.einsum("shd,hde->she", seg_query, memory, precision=lax.Precision.HIGHEST)
        )
        errors = (
            jnp.einsum("shd,hde->she", seg_keys, memory, precision=lax.Precision.HIGHEST)
            - seg_values
        )
        update = jnp.einsum("shd,she->hde", seg_keys, errors, precision=lax.Precision.HIGHEST)
        memory = (
            decay[0, segment][:, None, None] * memory - rate[0, segment][:, None, None] * update
        )
    recalled = jnp.concatenate(outputs, axis=0)
    combined = (attended + gate_open * recalled).reshape(length, local_width).astype(jnp.bfloat16)
    output_terms = lax.dot_general(
        combined, gathered[4], (((1,), (1,)), ((), ())), preferred_element_type=jnp.float32
    )
    summed = lax.psum_scatter(
        output_terms.astype(jnp.bfloat16), "col", scatter_dimension=1, tiled=True
    ).astype(jnp.float32)
    own_cols = lax.dynamic_slice_in_dim(xfloat, column * summed.shape[1], summed.shape[1], 1)
    mixed = (own_cols + summed).astype(jnp.bfloat16)
    return (mixed, memory[None])


def solution(mesh):
    return jax.shard_map(
        shards,
        mesh=mesh,
        in_specs=(
            P(("req", "row"), None),
            P(),
            P(None, "row", "col"),
            P(None, None, "col"),
            P(("req", "row"), None, None, None, None, "col"),
            P(),
            P(("req", "row"), "col", None, None),
            P(("req", "row"), None, "col"),
            P(("req", "row"), None, "col"),
        ),
        out_specs=(P(("req", "row"), "col"), P(("req", "row"), "col", None, None)),
        check_vma=False,
    )
```

profile of v0, /device:TPU:1, one launch (start us, length us, event | category | flops | bytes accessed | tf_op | source)
XLA Modules:
  0.0 468.3 jit_solution(4142681741803543050)
XLA Ops:
  7.2 2.2 copy.50
  9.4 1.5 multiply_reduce_fusion.1
  11.0 39.1 %all-gather.3.cloned.1.call-done = bf16[5,1024,256]{1,2,0:T(8,128)(2,1)} async-done(((bf16[5,256,256]{1,2,0:T(8,128)(2,1)}), bf16[5,1024,256]{1,2,0:T(8,128)(2,1)}) %all-gather.3.cloned.1.call-update) | async-done | bytes 2621456 | tf_op jit(solution)/shard_map/all_gather | solution.py:53
  50.0 3.3 fusion.109
  53.3 1.4 copy-done.9
  54.7 0.8 copy.56
  55.6 21.0 %copy.57 = bf16[1,32,1,256,2,256]{3,5,1,4,2,0:T(8,128)(2,1)} copy(bf16[1,32,1,256,2,256]{5,4,3,2,1,0:T(2,128)(2,1)} %param.13) | data formatting | bytes 16777216 | tf_op args[4]
  76.7 6.0 %fusion.106 = (bf16[32,1,256,1,256]{2,4,0,3,1:T(8,128)(2,1)}, bf16[32,1,256,1,256]{2,4,0,3,1:T(8,128)(2,1)}) fusion(bf16[32,1,256,2,256]{2,4,0,3,1:T(8,128)(2,1)} %bitcast.129), kind=kLoop, calls=%fused_computation.168 | loop fusion | bytes 16777216 | tf_op jit(solution)/shard_map/slice | solution.py:76
  82.7 28.5 %all-gather.5.cloned.1.call-done = bf16[32,512,2,128]{3,1,2,0:T(8,128)(2,1)} async-done(((bf16[1,512,2,128]{3,1,2,0:T(8,128)(2,1)}), bf16[32,512,2,128]{3,1,2,0:T(8,128)(2,1)}) %all-gather.5.cloned.1.call-update) | async-done | bytes 8388624 | tf_op jit(solution)/shard_map/all_gather | solution.py:72
  111.2 18.0 %fusion = (f32[32,2,512]{2,1,0:T(2,128)}, f32[32,2,512,256]{2,3,1,0:T(8,128)}) fusion(pred[32,256]{1,0:T(8,128)(4,1)S(1)} %add_compare_fusion, bf16[32,512,2,128]{3,1,2,0:T(8,128)(2,1)} %all-gather.5.cloned.1.call-done, bf16[32,256,2,128]{1,3,2,0:T(8,128)(2,1)} %bitcast.130), kind=kOutput, calls=%fused_computation.2 | convolution fusion | flops 2172616704 | bytes 46276608 | tf_op jit(solution)/shard_map/...shd,...khd->...hsk/dot_general | solution.py:15
  129.2 5.5 %all-to-all-start = ((f32[32,512,2]{1,2,0:T(2,128)}), f32[32,512,2]{1,2,0:T(2,128)S(1)}, u32[]{:S(2)}, u32[]{:S(2)}) async-start(f32[32,512,2]{1,2,0:T(2,128)} %bitcast.10), calls=%async_computation | async-start | bytes 262144 | tf_op jit(solution)/shard_map/all_to_all | solution.py:81
  134.7 16.1 %fusion.1 = f32[32,2,512]{2,1,0:T(2,128)} fusion(f32[32,2,512,256]{2,3,1,0:T(8,128)} %get-tuple-element.34, f32[32,2,512]{2,1,0:T(2,128)} %get-tuple-element.33, pred[32,256]{1,0:T(8,128)(4,1)S(1)} %add_compare_fusion), kind=kLoop, calls=%fused_computation.3 | loop fusion | flops 41910272 | bytes 33824768 | tf_op jit(solution)/shard_map/reduce_sum | solution.py:22
  150.8 7.4 %all-to-all-start.2 = ((f32[32,512,2]{1,2,0:T(2,128)}), f32[32,512,2]{1,2,0:T(2,128)S(1)}, u32[]{:S(2)}, u32[]{:S(2)}) async-start(f32[32,512,2]{1,2,0:T(2,128)} %bitcast.14), calls=%async_computation.2 | async-start | bytes 262144 | tf_op jit(solution)/shard_map/all_to_all | solution.py:82
  158.2 22.5 %fusion.10 = f32[32,512,2,128]{3,1,2,0:T(8,128)} fusion(bf16[32,256,2,128]{1,3,2,0:T(8,128)(2,1)} %bitcast.131, f32[32,2,512,256]{2,3,1,0:T(8,128)} %get-tuple-element.34, f32[32,2,512]{2,1,0:T(2,128)} %get-tuple-element.33, pred[32,256]{1,0:T(8,128)(4,1)S(1)} %add_compare_fusion), kind=kOutput, calls=%fused_computation.12 | convolution fusion | flops 2189426688 | bytes 54665216 | tf_op jit(solution)/shard_map/...hsk,...khd->...shd/dot_general | solution.py:23
  180.7 0.6 copy-done.7
  181.4 7.4 %all-to-all-start.1 = ((f32[32,512,2,128]{3,1,2,0:T(8,128)}), f32[32,512,2,128]{3,1,2,0:T(8,128)}, u32[]{:S(2)}, u32[]{:S(2)}) async-start(f32[32,512,2,128]{3,1,2,0:T(8,128)} %fusion.10), calls=%async_computation.1 | async-start | bytes 33554432 | tf_op jit(solution)/shard_map/all_to_all | solution.py:80
  189.0 0.7 concatenate.13
  192.9 1.1 fusion.41
  194.1 1.2 convolution_bitcast_fusion.7
  195.3 1.2 fusion.27
  196.6 1.2 fusion.40
  197.7 1.2 convolution_bitcast_fusion.6
  199.0 1.2 fusion.28
  200.2 1.1 fusion.39
  201.4 1.2 convolution_bitcast_fusion.5
  202.6 1.2 fusion.29
  203.8 1.1 fusion.38
  205.0 1.2 convolution_bitcast_fusion.4
  206.2 1.2 fusion.30
  207.5 1.1 fusion.37
  208.6 1.2 convolution_bitcast_fusion.3
  209.8 1.2 fusion.31
  211.1 1.1 fusion.36
  212.2 1.2 convolution_bitcast_fusion.2
  213.4 1.2 fusion.32
  214.7 1.2 convolution_bitcast_fusion.1
  215.9 1.0 concatenate.15
  217.0 2.0 fusion.57
  219.5 0.6 fusion.19
  220.3 189.0 %all-to-all-done.1 = f32[32,512,2,128]{3,1,2,0:T(8,128)} async-done(((f32[32,512,2,128]{3,1,2,0:T(8,128)}), f32[32,512,2,128]{3,1,2,0:T(8,128)}, u32[]{:S(2)}, u32[]{:S(2)}) %all-to-all-start.1) | async-done | bytes 16777248 | tf_op jit(solution)/shard_map/all_to_all | solution.py:80
  409.3 7.6 %multiply_reduce_fusion = f32[512,2,128]{2,0,1:T(8,128)S(1)} fusion(f32[32,512,2,128]{3,1,2,0:T(8,128)} %all-to-all-done.1, f32[32,512,2]{1,2,0:T(2,128)S(1)} %get-tuple-element.22), kind=kLoop, calls=%fused_computation.6 | loop fusion | flops 8257536 | bytes 17432576 | tf_op jit(solution)/shard_map/reduce_sum | solution.py:87
  416.9 1.0 copy.61
  417.9 2.5 fusion.25
  420.4 2.5 convolution_convert_fusion
  423.2 1.1 fusion.35
  424.4 1.9 fusion.34
  426.3 33.8 %reduce-scatter.2.cloned.1.call-done = bf16[512,256]{1,0:T(8,128)(2,1)} async-done(((bf16[512,1024]{1,0:T(8,128)(2,1)}), bf16[512,256]{1,0:T(8,128)(2,1)}) %reduce-scatter.2.cloned.1.call-update) | async-done | bytes 262160 | tf_op jit(solution)/shard_map/reduce_scatter | solution.py:123
  460.0 1.7 add_convert_fusion
  (64 shorter events, 4.5 us)
Async XLA Ops:
  7.2 42.9 %all-gather.3.cloned.1.call-start = ((), (), s32[]{:S(2)}) async-start(), calls=%async_computation.4 | async-start | bytes 3276800 | tf_op jit(solution)/shard_map/all_gather | solution.py:53
  9.4 101.8 %all-gather.5.cloned.1.call-start = ((), (), s32[]{:S(2)}) async-start(), calls=%async_computation.5 | async-start | bytes 8650752 | tf_op jit(solution)/shard_map/all_gather | solution.py:72
  53.3 1.4 copy-start.9
  55.6 21.0 %copy-start.13 = (s32[32]{0:T(128)S(1)}, s32[32]{0:T(128)}, u32[]{:S(2)}) copy-start(s32[32]{0:T(128)} %param.14) | copy-start | bytes 388
  129.2 21.6 %all-to-all-start = ((f32[32,512,2]{1,2,0:T(2,128)}), f32[32,512,2]{1,2,0:T(2,128)S(1)}, u32[]{:S(2)}, u32[]{:S(2)}) async-start(f32[32,512,2]{1,2,0:T(2,128)} %bitcast.10), calls=%async_computation | async-start | bytes 262144 | tf_op jit(solution)/shard_map/all_to_all | solution.py:81
  150.8 29.9 %all-to-all-start.2 = ((f32[32,512,2]{1,2,0:T(2,128)}), f32[32,512,2]{1,2,0:T(2,128)S(1)}, u32[]{:S(2)}, u32[]{:S(2)}) async-start(f32[32,512,2]{1,2,0:T(2,128)} %bitcast.14), calls=%async_computation.2 | async-start | bytes 262144 | tf_op jit(solution)/shard_map/all_to_all | solution.py:82
  180.7 8.2 %copy-start.12 = (bf16[2,16,256]{2,1,0:T(8,128)(2,1)S(1)}, bf16[2,16,256]{2,1,0:T(8,128)(2,1)}, u32[]{:S(2)}) copy-start(bf16[2,16,256]{2,1,0:T(8,128)(2,1)} %param.12) | copy-start | bytes 49156
  180.7 9.1 %copy-start.10 = (f32[1,8,2]{1,2,0:T(2,128)S(1)}, f32[1,8,2]{1,2,0:T(2,128)}, u32[]{:S(2)}) copy-start(f32[1,8,2]{1,2,0:T(2,128)} %param.17) | copy-start | bytes 196
  180.7 9.1 %copy-start.11 = (f32[1,8,2]{1,2,0:T(2,128)S(1)}, f32[1,8,2]{1,2,0:T(2,128)}, u32[]{:S(2)}) copy-start(f32[1,8,2]{1,2,0:T(2,128)} %param.16) | copy-start | bytes 196
  180.7 0.7 copy-start.7
  181.4 227.9 %all-to-all-start.1 = ((f32[32,512,2,128]{3,1,2,0:T(8,128)}), f32[32,512,2,128]{3,1,2,0:T(8,128)}, u32[]{:S(2)}, u32[]{:S(2)}) async-start(f32[32,512,2,128]{3,1,2,0:T(8,128)} %fusion.10), calls=%async_computation.1 | async-start | bytes 33554432 | tf_op jit(solution)/shard_map/all_to_all | solution.py:80
  188.8 2.7 copy-start.4
  188.8 271.2 %reduce-scatter.2.cloned.1.call-start = ((), (), s32[]{:S(2)}) async-start(), calls=%async_computation.6 | async-start | bytes 1310720 | tf_op jit(solution)/shard_map/reduce_scatter | solution.py:123
  190.4 1.1 copy-start.6
  190.8 2.0 copy-start.2
  191.5 2.5 copy-start.3
  192.1 0.8 copy-start
  196.6 22.4 %copy-start.5 = (pred[512,528]{0,1:T(8,128)(4,1)S(1)}, pred[512,528]{0,1:T(8,128)(4,1)}, u32[]{:S(2)}) copy-start(pred[512,528]{0,1:T(8,128)(4,1)} %concatenate.13) | copy-start | bytes 811012
  215.9 4.2 copy-start.8
  417.9 5.0 %copy-start.1 = (bf16[512,1024]{1,0:T(8,128)(2,1)S(1)}, bf16[512,1024]{1,0:T(8,128)(2,1)}, u32[]{:S(2)}) copy-start(bf16[512,1024]{1,0:T(8,128)(2,1)} %param.9) | copy-start | bytes 3145732
Sparse Core Ops, SparseCore 0:
  9.6 40.3 all-gather.2
  55.7 55.4 all-gather.4
  423.1 36.8 reduce-scatter.1
where the time goes:
time: 471 us; the launch traced here: 468 us
  waiting for transfers between devices  290 us (62%)
  matrix products  76.2 us (16%)
  local copies, waits for them, and re-layouts  36 us (8%)
  other arithmetic  31 us (7%)
  starting transfers between devices  20.4 us (4%)
  between operations  14.2 us (3%)
    all_to_all x1, waiting for transfers between devices, shards(): lax.all_to_all(part_out, ('req', 'row'), split_axis=0, concat_axis=0, til...  189 us
    all_gather x1, waiting for transfers between devices, shards(): gathered = lax.all_gather(w_attn, 'row', axis=1, tiled=True)  39.1 us
    reduce_scatter x1, waiting for transfers between devices, shards(): lax.psum_scatter(output_terms.astype(jnp.bfloat16), 'col', scatter_dimens...  33.8 us
    all_gather x1, waiting for transfers between devices, shards(): everyone = lax.all_gather(queries[None], ('req', 'row'), axis=0, tiled=True)  28.5 us
    unnamed x30, local copies, waits for them, and re-layouts  25.3 us
    dot_general x2, matrix products, attend(): jnp.einsum('...hsk,...khd->...shd', probabilities.astype(jnp.bfloat16), v...  25 us
    dot_general x2, matrix products, attend(): jnp.einsum('...shd,...khd->...hsk', query_heads, key_heads, preferred_ele...  18.5 us
    reduce_sum x2, other arithmetic, attend(): totals = jnp.sum(probabilities, axis=-1)  16.6 us
  transfers between devices with their start and end apart: 6, of which 4 were waited for; matrix products, arithmetic and copies ran while one was open for 22% of the time, Pallas kernels for 0%

commit v1 on v0

v1 whole, which is shorter than its diff:
```python
import jax
import jax.numpy as jnp
from jax import lax
from jax.experimental import pallas as pl
from jax.experimental.pallas import tpu as pltpu
from jax.sharding import PartitionSpec as P

HD = 128
NP = 16
SEG = 64
NEG = -1e30
LOG2E = 1.4426950408889634
SCALE = HD ** (-0.5) * LOG2E
F32 = jnp.float32
BF16 = jnp.bfloat16
MESH = pl.DeviceIdType.MESH
HIGH = lax.Precision.HIGHEST
BATCH = 8


def dot(a, b):
    return jnp.dot(a, b, preferred_element_type=F32)


def kernel(
    tok_hbm, gain_ref, w_hbm, persist_hbm, kv_hbm, clen_ref, state_hbm, dr_hbm,
    mixed_ref, newstate_ref,
    tok, normed, wfull, raw, wide, k_own, v_own, k_par, v_par, k_out, v_out,
    qbuf, obuf, sbuf, far_o, far_s, near_o, near_s, loc_o, loc_s,
    keys, vals, valst, gate_t, qun, kun, recall, mem, memt, dr, persist,
    comb, comb_all, w4all, state_in,
    l_sem, p_send, p_recv, w_send, w_recv, kv_send, kv_recv,
    ag_send, ag_recv, rs_send, rs_recv, x4_send, x4_recv, xc_send, xc_recv,
):
    req = lax.axis_index("req")
    z = lax.axis_index("row")
    x = lax.axis_index("col")
    y = req // 2
    k = req % 2
    other = 1 - k

    def at(dx=0, dy=0, dz=0, flip=False):
        core = other if flip else k
        return (((y + dy) % 4) * 2 + core, (z + dz) % 4, (x + dx) % 4)

    def push(src, dst, ssem, rsem, dev):
        copy = pltpu.make_async_remote_copy(
            src_ref=src, dst_ref=dst, send_sem=ssem, recv_sem=rsem,
            device_id=dev, device_id_type=MESH,
        )
        copy.start()
        return copy

    sent = []

    def send(src, dst, ssem, rsem, dev):
        sent.append(push(src, dst, ssem, rsem, dev))

    def arrive(dst, rsem):
        pltpu.make_async_copy(dst, dst, rsem).wait()

    lane = pl.ds(pl.multiple_of(k * HD, HD), HD)
    my_rows = pl.ds(pl.multiple_of(z * 256, 256), 256)
    local = [
        pltpu.make_async_copy(tok_hbm, tok.at[0], l_sem.at[0]),
        pltpu.make_async_copy(w_hbm.at[:, :, lane], wfull.at[:, my_rows, :], l_sem.at[1]),
        pltpu.make_async_copy(persist_hbm.at[:, :, lane], persist, l_sem.at[2]),
        pltpu.make_async_copy(state_hbm.at[k], state_in.at[0], l_sem.at[3]),
        pltpu.make_async_copy(dr_hbm.at[k], dr.at[0], l_sem.at[4]),
    ]
    pages = [
        pltpu.make_async_copy(
            kv_hbm.at[pl.ds(i * BATCH, BATCH)], raw.at[pl.ds(i * BATCH, BATCH)], l_sem.at[5 + i]
        )
        for i in range(4)
    ]
    for c in local:
        c.start()
    for c in pages:
        c.start()

    barrier = pltpu.get_barrier_semaphore()
    peers = [at(flip=True), at(dy=1), at(dy=3), at(dz=1), at(dz=3)]
    for d in (1, 2, 3):
        peers += [at(dx=d), at(dx=d, flip=True)]
    for dev in peers:
        pl.semaphore_signal(barrier, inc=1, device_id=dev, device_id_type=MESH)
    pl.semaphore_wait(barrier, len(peers))

    partner = at(flip=True)
    send(tok_hbm, tok.at[1], p_send.at[0], p_recv.at[0], partner)
    for g, (lo, n) in enumerate(((0, 1), (1, 4))):
        rows = w_hbm.at[pl.ds(lo, n), :, lane]
        land = wfull.at[pl.ds(lo, n), my_rows, :]
        send(rows, land, w_send.at[g, 0], w_recv.at[g, 0], at(dz=1))
        send(rows, land, w_send.at[g, 1], w_recv.at[g, 1], at(dz=3))
    send(state_hbm.at[other], state_in.at[1], p_send.at[1], p_recv.at[1], partner)
    send(dr_hbm.at[other], dr.at[1], p_send.at[2], p_recv.at[2], partner)

    below = pl.multiple_of(((z + 3) % 4) * 256, 256)
    above = pl.multiple_of(((z + 1) % 4) * 256, 256)
    far = pl.multiple_of(((z + 2) % 4) * 256, 256)

    def whole(g, start):
        lo, n = ((0, 1), (1, 4))[g]
        return wfull.at[pl.ds(lo, n), pl.ds(start, 256), :]

    def half(g, start, up):
        if g == 0:
            return wfull.at[pl.ds(0, 1), pl.ds(start + (0 if up else 128), 128), :]
        return wfull.at[pl.ds(1 if up else 3, 2), pl.ds(start, 256), :]

    def weights_forward(g):
        arrive(whole(g, below), w_recv.at[g, 0])
        send(half(g, below, True), half(g, below, True), w_send.at[g, 2], w_recv.at[g, 2], at(dz=1))
        arrive(whole(g, above), w_recv.at[g, 1])
        send(half(g, above, False), half(g, above, False), w_send.at[g, 3], w_recv.at[g, 3], at(dz=3))

    def weights_ready(g):
        arrive(half(g, far, True), w_recv.at[g, 2])
        arrive(half(g, far, False), w_recv.at[g, 3])

    def page(c):
        wide[...] = raw[c].astype(F32)
        k_own[c] = wide[pl.ds(2 * k, 256, stride=4), :].astype(BF16)
        v_own[c] = wide[pl.ds(2 * k + 1, 256, stride=4), :].T.astype(BF16)
        k_out[c] = wide[pl.ds(2 * other, 256, stride=4), :].astype(BF16)
        v_out[c] = wide[pl.ds(2 * other + 1, 256, stride=4), :].T.astype(BF16)

    def page_batch(i):
        pages[i].wait()

        def body(n, carry):
            page(i * BATCH + n)
            return carry

        lax.fori_loop(0, BATCH, body, 0)
        span = pl.ds(i * BATCH, BATCH)
        send(k_out.at[span], k_par.at[span], kv_send.at[i, 0], kv_recv.at[i, 0], partner)
        send(v_out.at[span], v_par.at[span], kv_send.at[i, 1], kv_recv.at[i, 1], partner)

    def norm(j):
        def body(n, carry):
            rows = pl.ds(pl.multiple_of(n * 128, 128), 128)
            v = tok[j, rows, :].astype(F32)
            s = lax.rsqrt(jnp.mean(v * v, axis=-1, keepdims=True) + 1e-05)
            normed[j, rows, :] = (v * s * gain_ref[...]).astype(BF16)
            return carry

        lax.fori_loop(0, 4, body, 0)

    local[0].wait()
    norm(0)
    page_batch(0)
    arrive(tok.at[1], p_recv.at[0])
    norm(1)
    weights_forward(0)
    page_batch(1)
    local[1].wait()
    weights_ready(0)

    def query_body(n, carry):
        j, h = n // 2, n % 2
        rows = pl.ds(pl.multiple_of(h * 256, 256), 256)
        q = dot(normed[j, rows, :], wfull[0])
        qbuf[h, 0, j] = q.T.astype(BF16)
        return carry

    lax.fori_loop(0, 4, query_body, 0)

    def step(h, axis, d):
        along_y = (h == 0) == (axis == 1)
        return at(dy=d) if along_y else at(dz=d)

    def ag_axis1_own():
        for h in (0, 1):
            send(qbuf.at[h, 0], qbuf.at[h, 12], ag_send.at[h, 0, 0], ag_recv.at[h, 12, 0], step(h, 1, 1))
            send(qbuf.at[h, 0], qbuf.at[h, 4], ag_send.at[h, 0, 1], ag_recv.at[h, 4, 0], step(h, 1, 3))

    def ag_axis1_forward():
        for h in (0, 1):
            arrive(qbuf.at[h, 12], ag_recv.at[h, 12, 0])
            send(qbuf.at[h, 12, 0], qbuf.at[h, 8, 0], ag_send.at[h, 12, 2], ag_recv.at[h, 8, 0], step(h, 1, 1))
            arrive(qbuf.at[h, 4], ag_recv.at[h, 4, 0])
            send(qbuf.at[h, 4, 1], qbuf.at[h, 8, 1], ag_send.at[h, 4, 2], ag_recv.at[h, 8, 1], step(h, 1, 3))

    def ag_axis2_own(d1):
        s = d1 * 4
        n = 2 if d1 == 0 else 0
        for h in (0, 1):
            send(qbuf.at[h, s], qbuf.at[h, s + 3], ag_send.at[h, s, n], ag_recv.at[h, s + 3, 0], step(h, 2, 1))
            send(qbuf.at[h, s], qbuf.at[h, s + 1], ag_send.at[h, s, n + 1], ag_recv.at[h, s + 1, 0], step(h, 2, 3))

    def ag_axis2_forward(d1):
        s = d1 * 4
        for h in (0, 1):
            arrive(qbuf.at[h, s + 3], ag_recv.at[h, s + 3, 0])
            send(qbuf.at[h, s + 3, 0], qbuf.at[h, s + 2, 0], ag_send.at[h, s + 3, 2], ag_recv.at[h, s + 2, 0], step(h, 2, 1))
            arrive(qbuf.at[h, s + 1], ag_recv.at[h, s + 1, 0])
            send(qbuf.at[h, s + 1, 1], qbuf.at[h, s + 2, 1], ag_send.at[h, s + 1, 2], ag_recv.at[h, s + 2, 1], step(h, 2, 3))

    def ag_far(s):
        for h in (0, 1):
            for j in (0, 1):
                arrive(qbuf.at[h, s, j], ag_recv.at[h, s, j])

    me = req * 4 + z
    partner_me = (2 * y + other) * 4 + z

    def tasks(count, first, second):
        def body(i, carry):
            n, h, j = i // 4, (i // 2) % 2, i % 2
            d1, d2 = first(n), second(n)
            slot = d1 * 4 + d2
            dy = d1 + h * (d2 - d1)
            dz = d2 + h * (d1 - d2)
            core = k + j * (1 - 2 * k)
            c = (((y + dy) % 4) * 2 + core) * 4 + (z + dz) % 4
            room = clen_ref[c]
            base0 = ((me - c + 32) % 32) * 256
            base1 = ((partner_me - c + 32) % 32) * 256
            q = qbuf[h, slot, j]
            pos = lax.broadcasted_iota(jnp.int32, (256, 256), 0)
            s0 = jnp.where(pos < room - base0, dot(k_own[c], q) * SCALE, NEG)
            s1 = jnp.where(pos < room - base1, dot(k_par[c], q) * SCALE, NEG)
            m = jnp.max(jnp.maximum(s0, s1), axis=0, keepdims=True)
            p0 = jnp.exp2(s0 - m)
            p1 = jnp.exp2(s1 - m)
            total = jnp.sum(p0 + p1, axis=0, keepdims=True)
            out = dot(v_own[c], p0.astype(BF16)) + dot(v_par[c], p1.astype(BF16))
            obuf[h, slot, j] = out.astype(BF16)
            sbuf[h, slot, j, 0:1, :] = m
            sbuf[h, slot, j, 1:2, :] = total
            return carry

        lax.fori_loop(0, 4 * count, body, 0)

    ag_axis1_own()
    ag_axis2_own(0)
    page_batch(2)
    page_batch(3)
    ag_axis1_forward()
    ag_axis2_own(3)
    ag_axis2_own(1)
    for i in range(4):
        span = pl.ds(i * BATCH, BATCH)
        arrive(k_par.at[span], kv_recv.at[i, 0])
        arrive(v_par.at[span], kv_recv.at[i, 1])
    tasks(1, lambda n: 0, lambda n: 0)
    ag_axis2_forward(0)
    ag_far(8)
    ag_axis2_own(2)
    tasks(2, lambda n: 3 - 2 * n, lambda n: 0)
    weights_forward(1)
    ag_axis2_forward(3)
    tasks(2, lambda n: 0, lambda n: 3 - 2 * n)
    ag_axis2_forward(1)
    tasks(1, lambda n: 2, lambda n: 0)
    tasks(2, lambda n: 3, lambda n: 3 - 2 * n)
    ag_axis2_forward(2)
    tasks(2, lambda n: 1, lambda n: 3 - 2 * n)
    ag_far(2)
    tasks(1, lambda n: 0, lambda n: 2)

    def slots(line):
        return (4, 8, 12) if line == 4 else (line * 4 + 1, line * 4 + 2, line * 4 + 3)

    def hop(h, line, d):
        return step(h, 1 if line == 4 else 2, d)

    def rs_far(line):
        s = slots(line)[1]
        for h in (0, 1):
            for j, d in ((0, 1), (1, 3)):
                send(obuf.at[h, s, j], far_o.at[h, line, j], rs_send.at[h, line, j, 0], rs_recv.at[h, line, j, 0], hop(h, line, d))
                send(sbuf.at[h, s, j], far_s.at[h, line, j], rs_send.at[h, line, j, 1], rs_recv.at[h, line, j, 1], hop(h, line, d))

    def merge(pieces):
        m = pieces[0][1][0:1, :]
        for _, st in pieces[1:]:
            m = jnp.maximum(m, st[0:1, :])
        total, out = None, None
        for o, st in pieces:
            f = jnp.exp2(st[0:1, :] - m)
            t = st[1:2, :] * f
            w = o.astype(F32) * f
            total = t if total is None else total + t
            out = w if out is None else out + w
        return out, m, total

    def put(h, slot, j, merged):
        out, m, total = merged
        obuf[h, slot, j] = out.astype(BF16)
        sbuf[h, slot, j, 0:1, :] = m
        sbuf[h, slot, j, 1:2, :] = total

    def rs_near(line):
        for h in (0, 1):
            for j in (0, 1):
                arrive(far_o.at[h, line, j], rs_recv.at[h, line, j, 0])
                arrive(far_s.at[h, line, j], rs_recv.at[h, line, j, 1])
        first, _, last = slots(line)

        def body(i, carry):
            h, j = i // 2, i % 2
            slot = first + j * (last - first)
            put(h, slot, j, merge([(obuf[h, slot, j], sbuf[h, slot, j]), (far_o[h, line, j], far_s[h, line, j])]))
            return carry

        lax.fori_loop(0, 4, body, 0)
        for h in (0, 1):
            for side, (s, d) in enumerate(((first, 1), (last, 3))):
                send(obuf.at[h, s], near_o.at[h, line, side], rs_send.at[h, line, 2 + side, 0], rs_recv.at[h, line, 2 + side, 0], hop(h, line, d))
                send(sbuf.at[h, s], near_s.at[h, line, side], rs_send.at[h, line, 2 + side, 1], rs_recv.at[h, line, 2 + side, 1], hop(h, line, d))

    def near_ready(line):
        for h in (0, 1):
            for side in (0, 1):
                arrive(near_o.at[h, line, side], rs_recv.at[h, line, 2 + side, 0])
                arrive(near_s.at[h, line, side], rs_recv.at[h, line, 2 + side, 1])

    def rs_column(line):
        near_ready(line)

        def body(i, carry):
            h, j = i // 2, i % 2
            slot = line * 4
            put(h, slot, j, merge([
                (obuf[h, slot, j], sbuf[h, slot, j]),
                (near_o[h, line, 0, j], near_s[h, line, 0, j]),
                (near_o[h, line, 1, j], near_s[h, line, 1, j]),
            ]))
            return carry

        lax.fori_loop(0, 4, body, 0)

    rs_far(0)
    tasks(2, lambda n: 2, lambda n: 3 - 2 * n)
    ag_far(14)
    ag_far(6)
    tasks(2, lambda n: 3 - 2 * n, lambda n: 2)
    rs_far(3)
    rs_far(1)
    ag_far(10)
    tasks(1, lambda n: 2, lambda n: 2)
    rs_far(2)

    weights_ready(1)

    def project_body(n, carry):
        j, h = n // 2, n % 2
        rows = pl.ds(pl.multiple_of(h * 256, 256), 256)
        nb = normed[j, rows, :]
        kk = dot(nb, wfull[1]).astype(BF16)
        vv = dot(nb, wfull[2]).astype(BF16)
        keys[j, rows, :] = kk
        vals[j, rows, :] = vv.astype(F32)
        valst[j, h] = vv.astype(F32).T.astype(BF16)
        gate_t[j, h] = jax.nn.sigmoid(dot(nb, wfull[3]).T)
        kf = kk.astype(F32)
        kun[j, rows, :] = kf * lax.rsqrt(jnp.sum(kf * kf, axis=-1, keepdims=True) + 1e-06)
        qf = qbuf[h, 0, j].astype(F32)
        qun[j, h] = qf * lax.rsqrt(jnp.sum(qf * qf, axis=0, keepdims=True) + 1e-06)
        return carry

    lax.fori_loop(0, 4, project_body, 0)

    head = 2 * x + k
    n = 0
    for d in (1, 2, 3):
        cols = pl.ds(pl.multiple_of(((x + d) % 4) * 256, 256), 256)
        for flip in (False, True):
            send(wfull.at[4, cols, :], w4all.at[head], x4_send.at[n], x4_recv.at[d, k], at(dx=d, flip=flip))
            n += 1
    mine = pl.ds(pl.multiple_of(x * 256, 256), 256)
    send(wfull.at[4, mine, :], w4all.at[head], x4_send.at[6], x4_recv.at[0, k], partner)

    rs_near(2)
    local[2].wait()
    w4all[head] = wfull[4, mine, :]

    def own_body(i, carry):
        h, j = i // 2, i % 2
        q = qbuf[h, 0, j]
        token = lax.broadcasted_iota(jnp.int32, (512, 256), 1) + h * 256
        place = lax.broadcasted_iota(jnp.int32, (512, 256), 0)
        s = jnp.where(place <= token, dot(keys[j], q) * SCALE, NEG)
        sp = dot(persist[0], q) * SCALE
        m = jnp.maximum(jnp.max(s, axis=0, keepdims=True), jnp.max(sp, axis=0, keepdims=True))
        p = jnp.exp2(s - m)
        pp = jnp.exp2(sp - m)
        total = jnp.sum(p, axis=0, keepdims=True) + jnp.sum(pp, axis=0, keepdims=True)
        pb = p.astype(BF16)
        out = dot(valst[j, 0], pb[:256]) + dot(valst[j, 1], pb[256:])
        out = out + lax.dot_general(persist[1], pp.astype(BF16), (((0,), (0,)), ((), ())), preferred_element_type=F32)
        loc_o[h, j] = out
        loc_s[h, j, 0:1, :] = m
        loc_s[h, j, 1:2, :] = total
        return carry

    lax.fori_loop(0, 4, own_body, 0)

    rs_near(3)
    rs_near(1)

    local[3].wait()
    local[4].wait()
    arrive(state_in.at[1], p_recv.at[1])
    arrive(dr.at[1], p_recv.at[2])
    for j in (0, 1):
        memt[j] = state_in[j].T

    def memory_body(t, carry):
        lanes = lax.broadcasted_iota(jnp.int32, (HD, HD), 1)
        for j in (0, 1):
            h, lo = t // 2, pl.multiple_of((t % 2) * HD, HD)
            q = qun[j, h, :, pl.ds(lo, HD)]
            parts = []
            for u in (0, 1):
                seg = 2 * t + u
                rows = pl.ds(pl.multiple_of(seg * SEG, SEG), SEG)
                kn = kun[j, rows, :]
                vs = vals[j, rows, :]
                m_now = memt[j]
                parts.append(jnp.dot(m_now, q, precision=HIGH, preferred_element_type=F32))
                gram = lax.dot_general(kn, kn, (((0,), (0,)), ((), ())), precision=HIGH, preferred_element_type=F32)
                target = lax.dot_general(vs, kn, (((0,), (0,)), ((), ())), precision=HIGH, preferred_element_type=F32)
                update = jnp.dot(m_now, gram, precision=HIGH, preferred_element_type=F32) - target
                memt[j] = dr[j, pl.ds(seg, 1), :] * m_now - dr[j, pl.ds(8 + seg, 1), :] * update
            recall[j, h, :, pl.ds(lo, HD)] = jnp.where(lanes < SEG, parts[0], parts[1])
        return carry

    lax.fori_loop(0, 4, memory_body, 0)
    for j in (0, 1):
        mem[j] = memt[j].T
    send(mem.at[1], state_in.at[2], p_send.at[3], p_recv.at[3], partner)

    rs_near(0)
    rs_column(2)
    rs_far(4)
    rs_column(3)
    rs_column(1)
    rs_near(4)
    near_ready(0)
    near_ready(4)

    def final_body(i, carry):
        h, j = i // 2, i % 2
        out, _, total = merge([
            (obuf[h, 0, j], sbuf[h, 0, j]),
            (near_o[h, 0, 0, j], near_s[h, 0, 0, j]),
            (near_o[h, 0, 1, j], near_s[h, 0, 1, j]),
            (near_o[h, 4, 0, j], near_s[h, 4, 0, j]),
            (near_o[h, 4, 1, j], near_s[h, 4, 1, j]),
            (loc_o[h, j], loc_s[h, j]),
        ])
        comb[h, j] = (out / total + gate_t[j, h] * recall[j, h]).astype(BF16)
        return carry

    lax.fori_loop(0, 4, final_body, 0)

    def slot_of(d, core):
        return ((x + d) % 4) * 2 + core

    for h in (0, 1):
        for n, (dx, flip) in enumerate(((1, False), (1, True), (3, False), (3, True), (0, True))):
            j = 1 if flip else 0
            send(comb.at[h, j], comb_all.at[h, head], xc_send.at[h, n], xc_recv.at[h, (4 - dx) % 4, k], at(dx=dx, flip=flip))
    for h in (0, 1):
        comb_all[h, head] = comb[h, 0]
    for h in (0, 1):
        for core in (0, 1):
            arrive(comb_all.at[h, slot_of(3, core)], xc_recv.at[h, 3, core])
            arrive(comb_all.at[h, slot_of(1, core)], xc_recv.at[h, 1, core])
        up, down = slot_of(3, 0), slot_of(1, 1)
        send(comb_all.at[h, up], comb_all.at[h, up], xc_send.at[h, 5], xc_recv.at[h, 2, 0], at(dx=1))
        send(comb_all.at[h, down], comb_all.at[h, down], xc_send.at[h, 6], xc_recv.at[h, 2, 1], at(dx=3))
    for d in (1, 2, 3):
        for core in (0, 1):
            arrive(w4all.at[slot_of(4 - d, core)], x4_recv.at[d, core])
    arrive(w4all.at[slot_of(0, other)], x4_recv.at[0, other])

    arrive(state_in.at[2], p_recv.at[3])
    newstate_ref[k] = mem[0]
    newstate_ref[other] = state_in[2]

    for h in (0, 1):
        arrive(comb_all.at[h, slot_of(0, other)], xc_recv.at[h, 0, other])
        for core in (0, 1):
            arrive(comb_all.at[h, slot_of(2, core)], xc_recv.at[h, 2, core])
        acc = dot(w4all[0], comb_all[h, 0])
        for g in range(1, 8):
            acc = acc + dot(w4all[g], comb_all[h, g])
        rows = pl.ds(h * 256, 256)
        resid = tok[0, rows, pl.ds(pl.multiple_of(x * 256, 256), 256)].astype(F32)
        mixed_ref[rows, :] = (resid + acc.T).astype(BF16)

    for c in sent:
        c.wait_send()


def shards(tokens, norm_gain, w_attn, persist_kv, kv_pool, cache_len, mem_state, decay, rate):
    kv = kv_pool.reshape(32, 256, 2, 2, HD).transpose(0, 1, 3, 2, 4).reshape(32, 1024, HD)
    dr = jnp.concatenate([decay[0], rate[0]], axis=0).T
    dr = jnp.broadcast_to(dr[:, :, None], (2, 16, HD))
    hbm = pl.BlockSpec(memory_space=pl.ANY)
    vmem = pl.BlockSpec(memory_space=pltpu.VMEM)
    V = pltpu.VMEM
    dma = pltpu.SemaphoreType.DMA
    mixed, new_state = pl.pallas_call(
        kernel,
        out_shape=(
            jax.ShapeDtypeStruct((512, 256), BF16),
            jax.ShapeDtypeStruct((2, HD, HD), F32),
        ),
        in_specs=[hbm, vmem, hbm, hbm, hbm, pl.BlockSpec(memory_space=pltpu.SMEM), hbm, hbm],
        out_specs=(vmem, vmem),
        scratch_shapes=[
            V((2, 512, 1024), BF16),
            V((2, 512, 1024), BF16),
            V((5, 1024, HD), BF16),
            V((32, 1024, HD), BF16),
            V((1024, HD), F32),
            V((32, 256, HD), BF16), V((32, HD, 256), BF16),
            V((32, 256, HD), BF16), V((32, HD, 256), BF16),
            V((32, 256, HD), BF16), V((32, HD, 256), BF16),
            V((2, 16, 2, HD, 256), BF16),
            V((2, 16, 2, HD, 256), BF16),
            V((2, 16, 2, 2, 256), F32),
            V((2, 5, 2, HD, 256), BF16), V((2, 5, 2, 2, 256), F32),
            V((2, 5, 2, 2, HD, 256), BF16), V((2, 5, 2, 2, 2, 256), F32),
            V((2, 2, HD, 256), F32), V((2, 2, 2, 256), F32),
            V((2, 512, HD), BF16), V((2, 512, HD), F32), V((2, 2, HD, 256), BF16),
            V((2, 2, HD, 256), F32), V((2, 2, HD, 256), F32), V((2, 512, HD), F32),
            V((2, 2, HD, 256), F32),
            V((2, HD, HD), F32), V((2, HD, HD), F32),
            V((2, 16, HD), F32), V((2, NP, HD), BF16),
            V((2, 2, HD, 256), BF16), V((2, 8, HD, 256), BF16),
            V((8, 256, HD), BF16),
            V((3, HD, HD), F32),
            dma((9,)), dma((4,)), dma((4,)), dma((2, 4)), dma((2, 4)), dma((4, 2)), dma((4, 2)),
            dma((2, 16, 4)), dma((2, 16, 2)), dma((2, 5, 4, 2)), dma((2, 5, 4, 2)),
            dma((7,)), dma((4, 2)), dma((2, 7)), dma((2, 4, 2)),
        ],
        compiler_params=pltpu.CompilerParams(
            collective_id=0, has_side_effects=True, vmem_limit_bytes=60 * 1024 * 1024
        ),
        name="prefill",
    )(tokens, norm_gain[None], w_attn, persist_kv, kv, cache_len, mem_state[0], dr)
    return (mixed, new_state[None])


def solution(mesh):
    return jax.shard_map(
        shards,
        mesh=mesh,
        in_specs=(
            P(("req", "row"), None),
            P(),
            P(None, "row", "col"),
            P(None, None, "col"),
            P(("req", "row"), None, None, None, None, "col"),
            P(),
            P(("req", "row"), "col", None, None),
            P(("req", "row"), None, "col"),
            P(("req", "row"), None, "col"),
        ),
        out_specs=(P(("req", "row"), "col"), P(("req", "row"), "col", None, None)),
        check_vma=False,
    )
```

time: 471 us -> 110 us (0.23)
  waiting for transfers between devices: 290 us -> 0 us
  Pallas kernels: 0 us -> 105 us
  matrix products: 76.2 us -> 0 us
  local copies, waits for them, and re-layouts: 36 us -> 3.91 us
  other arithmetic: 31 us -> 0.77 us
  starting transfers between devices: 20.4 us -> 0 us
  between operations: 14.2 us -> 0.64 us
    all_to_all x3 -> x0, waiting for transfers between devices: 189 us -> none  [the longest x1 189 us: shards(): lax.all_to_all(part_out, ('req', 'row'), split_axis=0, concat_axis=0, til...]
    pallas_call x0 -> x1, Pallas kernels: none -> 105 us  [shards(): pl.pallas_call(kernel, out_shape=(jax.ShapeDtypeStruct((512, 256), BF16),...]
    dot_general x30 -> x0, matrix products: 76.2 us -> none  [the longest x2 25 us: attend(): jnp.einsum('...hsk,...khd->...shd', probabilities.astype(jnp.bfloat16), v...]
    all_gather x2 -> x0, waiting for transfers between devices: 67.6 us -> none  [the longest x1 39.1 us: shards(): gathered = lax.all_gather(w_attn, 'row', axis=1, tiled=True)]
    reduce_scatter x1 -> x0, waiting for transfers between devices: 33.8 us -> none  [shards(): lax.psum_scatter(output_terms.astype(jnp.bfloat16), 'col', scatter_dimens...]
    reduce_sum x7 -> x0, other arithmetic: 26.3 us -> none  [the longest x2 16.6 us: attend(): totals = jnp.sum(probabilities, axis=-1)]
    unnamed x30 -> x2, local copies, waits for them, and re-layouts: 25.3 us -> 3.24 us
    all_to_all x3 -> x0, starting transfers between devices: 20.3 us -> none  [the longest x1 7.43 us: shards(): lax.all_to_all(part_out, ('req', 'row'), split_axis=0, concat_axis=0, til...]
  transfers between devices with their start and end apart: 6 -> 0, of which waited for: 4 -> 0; matrix products, arithmetic and copies ran while one was open for 22% -> 0% of each run, Pallas kernels for 0% -> 0%
where the time goes in v1:
time: 110 us
  Pallas kernels  105 us (95%)
  local copies, waits for them, and re-layouts  3.91 us (4%)
    pallas_call x1, Pallas kernels, shards(): pl.pallas_call(kernel, out_shape=(jax.ShapeDtypeStruct((512, 256), BF16),...  105 us
    unnamed x2, local copies, waits for them, and re-layouts  3.24 us

profile of v1, /device:TPU:1, one launch (start us, length us, event | category | flops | bytes accessed | tf_op | source)
XLA Modules:
  0.0 110.0 jit_solution(15024624740521190381)
XLA Ops:
  0.6 0.8 maximum_bitcast_fusion
  1.4 0.7 broadcast_in_dim.13.dr_hbm
  2.1 104.7 %prefill.1 = (bf16[512,256]{1,0:T(8,128)(2,1)}, f32[2,128,128]{2,1,0:T(8,128)}) custom-call(bf16[512,1024]{1,0:T(8,128)(2,1)} %tok_hbm.1, f32[1,1024]{1,0:T(1,128)} %bitcast.15, bf16[5,256,256]{2,1,0:T(8,128)(2,1)} %w_hbm.1, bf16[2,16,256]{2,1,0:T(8,128)(2,1)} %persist_hbm.1, bf16[32,1024,128]{2,1,0:T(8,128)(2,1)} %bitcast.12, s32[32]{0:T(128)} %clen_ref.1, ...), custom_call_target="tpu_custom_call" | custom-call | tf_op jit(solution)/shard_map/prefill/pallas_call | solution.py:510
  106.7 1.7 %copy.14 = bf16[512,256]{1,0:T(8,128)(2,1)} copy(bf16[512,256]{1,0:T(8,128)(2,1)} %get-tuple-element.8) | data formatting | bytes 524288
  108.4 1.6 %copy.15 = f32[1,2,128,128]{3,2,1,0:T(8,128)} copy(f32[1,2,128,128]{3,2,1,0:T(8,128)} %bitcast.14) | data formatting | bytes 262144

commit v2 on v1

--- a/solution.py
+++ b/solution.py
@@ -16,6 +16,8 @@
 MESH = pl.DeviceIdType.MESH
 HIGH = lax.Precision.HIGHEST
 BATCH = 8
+GROUPS = ((0, 1), (1, 3), (4, 1))
+VR = HD + 16
 
 
 def dot(a, b):
@@ -23,11 +25,11 @@
 
 
 def kernel(
-    tok_hbm, gain_ref, w_hbm, persist_hbm, kv_hbm, clen_ref, state_hbm, dr_hbm,
+    tok_hbm, gain_ref, w_hbm, persist_hbm, kv_hbm, clen_ref, state_hbm, decay_ref, rate_ref,
     mixed_ref, newstate_ref,
-    tok, normed, wfull, raw, wide, k_own, v_own, k_par, v_par, k_out, v_out,
+    tok, normed, wfull, raw, wide, k_own, v_own, k_par, v_par, k_out, v_out, bias,
     qbuf, obuf, sbuf, far_o, far_s, near_o, near_s, loc_o, loc_s,
-    keys, vals, valst, gate_t, qun, kun, recall, mem, memt, dr, persist,
+    keys, vals, valst, gate_t, qun, kun, recall, mem, memt, dr, dr_out, persist,
     comb, comb_all, w4all, state_in,
     l_sem, p_send, p_recv, w_send, w_recv, kv_send, kv_recv,
     ag_send, ag_recv, rs_send, rs_recv, x4_send, x4_recv, xc_send, xc_recv,
@@ -66,7 +68,6 @@
         pltpu.make_async_copy(w_hbm.at[:, :, lane], wfull.at[:, my_rows, :], l_sem.at[1]),
         pltpu.make_async_copy(persist_hbm.at[:, :, lane], persist, l_sem.at[2]),
         pltpu.make_async_copy(state_hbm.at[k], state_in.at[0], l_sem.at[3]),
-        pltpu.make_async_copy(dr_hbm.at[k], dr.at[0], l_sem.at[4]),
     ]
     pages = [
         pltpu.make_async_copy(
@@ -87,28 +88,35 @@
         pl.semaphore_signal(barrier, inc=1, device_id=dev, device_id_type=MESH)
     pl.semaphore_wait(barrier, len(peers))
 
-    partner = at(flip=True)
-    send(tok_hbm, tok.at[1], p_send.at[0], p_recv.at[0], partner)
-    for g, (lo, n) in enumerate(((0, 1), (1, 4))):
+    def weights_own(g):
+        lo, n = GROUPS[g]
         rows = w_hbm.at[pl.ds(lo, n), :, lane]
         land = wfull.at[pl.ds(lo, n), my_rows, :]
         send(rows, land, w_send.at[g, 0], w_recv.at[g, 0], at(dz=1))
         send(rows, land, w_send.at[g, 1], w_recv.at[g, 1], at(dz=3))
+
+    partner = at(flip=True)
+    weights_own(0)
+    send(tok_hbm, tok.at[1], p_send.at[0], p_recv.at[0], partner)
     send(state_hbm.at[other], state_in.at[1], p_send.at[1], p_recv.at[1], partner)
-    send(dr_hbm.at[other], dr.at[1], p_send.at[2], p_recv.at[2], partner)
+    for n in range(8):
+        for hh in (0, 1):
+            dr_out[hh, n : n + 1, :] = jnp.full((1, HD), decay_ref[hh, n], F32)
+            dr_out[hh, 8 + n : 9 + n, :] = jnp.full((1, HD), rate_ref[hh, n], F32)
+    send(dr_out.at[other], dr.at[1], p_send.at[2], p_recv.at[2], partner)
+    dr[0] = dr_out[k]
 
     below = pl.multiple_of(((z + 3) % 4) * 256, 256)
     above = pl.multiple_of(((z + 1) % 4) * 256, 256)
     far = pl.multiple_of(((z + 2) % 4) * 256, 256)
 
     def whole(g, start):
-        lo, n = ((0, 1), (1, 4))[g]
+        lo, n = GROUPS[g]
         return wfull.at[pl.ds(lo, n), pl.ds(start, 256), :]
 
     def half(g, start, up):
-        if g == 0:
-            return wfull.at[pl.ds(0, 1), pl.ds(start + (0 if up else 128), 128), :]
-        return wfull.at[pl.ds(1 if up else 3, 2), pl.ds(start, 256), :]
+        lo, n = GROUPS[g]
+        return wfull.at[pl.ds(lo, n), pl.ds(start + (0 if up else 128), 128), :]
 
     def weights_forward(g):
         arrive(whole(g, below), w_recv.at[g, 0])
@@ -120,10 +128,19 @@
         arrive(half(g, far, True), w_recv.at[g, 2])
         arrive(half(g, far, False), w_recv.at[g, 3])
 
+    me = req * 4 + z
+    partner_me = (2 * y + other) * 4 + z
+
     def page(c):
+        place = lax.broadcasted_iota(jnp.int32, (256, HD), 0)
+        for i, pool in ((0, me), (1, partner_me)):
+            room = clen_ref[c] - ((pool - c + 32) % 32) * 256
+            bias[c, i] = jnp.where(place < room, 0.0, NEG)
+        v_own[c, HD:, :] = jnp.ones((16, 256), BF16)
+        v_par[c, HD:, :] = jnp.ones((16, 256), BF16)
         wide[...] = raw[c].astype(F32)
         k_own[c] = wide[pl.ds(2 * k, 256, stride=4), :].astype(BF16)
-        v_own[c] = wide[pl.ds(2 * k + 1, 256, stride=4), :].T.astype(BF16)
+        v_own[c, :HD, :] = wide[pl.ds(2 * k + 1, 256, stride=4), :].T.astype(BF16)
         k_out[c] = wide[pl.ds(2 * other, 256, stride=4), :].astype(BF16)
         v_out[c] = wide[pl.ds(2 * other + 1, 256, stride=4), :].T.astype(BF16)
 
@@ -137,7 +154,7 @@
         lax.fori_loop(0, BATCH, body, 0)
         span = pl.ds(i * BATCH, BATCH)
         send(k_out.at[span], k_par.at[span], kv_send.at[i, 0], kv_recv.at[i, 0], partner)
-        send(v_out.at[span], v_par.at[span], kv_send.at[i, 1], kv_recv.at[i, 1], partner)
+        send(v_out.at[span], v_par.at[span, pl.ds(0, HD)], kv_send.at[i, 1], kv_recv.at[i, 1], partner)
 
     def norm(j):
         def body(n, carry):
@@ -155,6 +172,7 @@
     arrive(tok.at[1], p_recv.at[0])
     norm(1)
     weights_forward(0)
+    weights_own(1)
     page_batch(1)
     local[1].wait()
     weights_ready(0)
@@ -204,36 +222,31 @@
             for j in (0, 1):
                 arrive(qbuf.at[h, s, j], ag_recv.at[h, s, j])
 
-    me = req * 4 + z
-    partner_me = (2 * y + other) * 4 + z
-
     def tasks(count, first, second):
         def body(i, carry):
-            n, h, j = i // 4, (i // 2) % 2, i % 2
+            n, h = i // 2, i % 2
             d1, d2 = first(n), second(n)
             slot = d1 * 4 + d2
             dy = d1 + h * (d2 - d1)
             dz = d2 + h * (d1 - d2)
-            core = k + j * (1 - 2 * k)
-            c = (((y + dy) % 4) * 2 + core) * 4 + (z + dz) % 4
-            room = clen_ref[c]
-            base0 = ((me - c + 32) % 32) * 256
-            base1 = ((partner_me - c + 32) % 32) * 256
-            q = qbuf[h, slot, j]
-            pos = lax.broadcasted_iota(jnp.int32, (256, 256), 0)
-            s0 = jnp.where(pos < room - base0, dot(k_own[c], q) * SCALE, NEG)
-            s1 = jnp.where(pos < room - base1, dot(k_par[c], q) * SCALE, NEG)
-            m = jnp.max(jnp.maximum(s0, s1), axis=0, keepdims=True)
-            p0 = jnp.exp2(s0 - m)
-            p1 = jnp.exp2(s1 - m)
-            total = jnp.sum(p0 + p1, axis=0, keepdims=True)
-            out = dot(v_own[c], p0.astype(BF16)) + dot(v_par[c], p1.astype(BF16))
-            obuf[h, slot, j] = out.astype(BF16)
-            sbuf[h, slot, j, 0:1, :] = m
-            sbuf[h, slot, j, 1:2, :] = total
+            blocks = [(((y + dy) % 4) * 2 + core) * 4 + (z + dz) % 4 for core in (k, other)]
+            scores = []
+            for j, c in enumerate(blocks):
+                q = qbuf[h, slot, j]
+                mask = [jnp.concatenate([bias[c, i]] * 2, axis=1) for i in (0, 1)]
+                scores.append((dot(k_own[c], q) + mask[0], dot(k_par[c], q) + mask[1]))
+            for j, c in enumerate(blocks):
+                s0, s1 = scores[j]
+                m = jnp.max(jnp.maximum(s0, s1), axis=0, keepdims=True)
+                p0 = jnp.exp2((s0 - m) * SCALE).astype(BF16)
+                p1 = jnp.exp2((s1 - m) * SCALE).astype(BF16)
+                out = dot(v_own[c], p0) + dot(v_par[c], p1)
+                obuf[h, slot, j] = out[:HD].astype(BF16)
+                sbuf[h, slot, j, 0:1, :] = m * SCALE
+                sbuf[h, slot, j, 1:2, :] = out[HD : HD + 1]
             return carry
 
-        lax.fori_loop(0, 4 * count, body, 0)
+        lax.fori_loop(0, 2 * count, body, 0)
 
     ag_axis1_own()
     ag_axis2_own(0)
@@ -241,24 +254,26 @@
     page_batch(3)
     ag_axis1_forward()
     ag_axis2_own(3)
-    ag_axis2_own(1)
     for i in range(4):
         span = pl.ds(i * BATCH, BATCH)
         arrive(k_par.at[span], kv_recv.at[i, 0])
-        arrive(v_par.at[span], kv_recv.at[i, 1])
+        arrive(v_par.at[span, pl.ds(0, HD)], kv_recv.at[i, 1])
     tasks(1, lambda n: 0, lambda n: 0)
-    ag_axis2_forward(0)
     ag_far(8)
     ag_axis2_own(2)
+    ag_axis2_own(1)
+    weights_forward(1)
+    weights_own(2)
     tasks(2, lambda n: 3 - 2 * n, lambda n: 0)
-    weights_forward(1)
+    ag_axis2_forward(0)
+    tasks(2, lambda n: 0, lambda n: 3 - 2 * n)
     ag_axis2_forward(3)
-    tasks(2, lambda n: 0, lambda n: 3 - 2 * n)
+    tasks(1, lambda n: 2, lambda n: 0)
+    ag_axis2_forward(2)
+    tasks(2, lambda n: 3, lambda n: 3 - 2 * n)
     ag_axis2_forward(1)
-    tasks(1, lambda n: 2, lambda n: 0)
-    tasks(2, lambda n: 3, lambda n: 3 - 2 * n)
-    ag_axis2_forward(2)
-    tasks(2, lambda n: 1, lambda n: 3 - 2 * n)
+    weights_forward(2)
+    tasks(2, lambda n: 2, lambda n: 3 - 2 * n)
     ag_far(2)
     tasks(1, lambda n: 0, lambda n: 2)
 
@@ -335,15 +350,16 @@
         lax.fori_loop(0, 4, body, 0)
 
     rs_far(0)
-    tasks(2, lambda n: 2, lambda n: 3 - 2 * n)
+    ag_far(10)
+    tasks(1, lambda n: 2, lambda n: 2)
+    rs_far(2)
+    tasks(2, lambda n: 1, lambda n: 3 - 2 * n)
     ag_far(14)
     ag_far(6)
     tasks(2, lambda n: 3 - 2 * n, lambda n: 2)
     rs_far(3)
     rs_far(1)
-    ag_far(10)
-    tasks(1, lambda n: 2, lambda n: 2)
-    rs_far(2)
+    rs_near(2)
 
     weights_ready(1)
 
@@ -364,6 +380,9 @@
         return carry
 
     lax.fori_loop(0, 4, project_body, 0)
+    rs_near(3)
+    rs_near(1)
+    weights_ready(2)
 
     head = 2 * x + k
     n = 0
@@ -375,7 +394,6 @@
     mine = pl.ds(pl.multiple_of(x * 256, 256), 256)
     send(wfull.at[4, mine, :], w4all.at[head], x4_send.at[6], x4_recv.at[0, k], partner)
 
-    rs_near(2)
     local[2].wait()
     w4all[head] = wfull[4, mine, :]
 
@@ -400,11 +418,11 @@
 
     lax.fori_loop(0, 4, own_body, 0)
 
-    rs_near(3)
-    rs_near(1)
+    rs_column(2)
+    rs_far(4)
+    rs_near(0)
 
     local[3].wait()
-    local[4].wait()
     arrive(state_in.at[1], p_recv.at[1])
     arrive(dr.at[1], p_recv.at[2])
     for j in (0, 1):
@@ -435,9 +453,6 @@
         mem[j] = memt[j].T
     send(mem.at[1], state_in.at[2], p_send.at[3], p_recv.at[3], partner)
 
-    rs_near(0)
-    rs_column(2)
-    rs_far(4)
     rs_column(3)
     rs_column(1)
     rs_near(4)
@@ -501,10 +516,9 @@
 
 def shards(tokens, norm_gain, w_attn, persist_kv, kv_pool, cache_len, mem_state, decay, rate):
     kv = kv_pool.reshape(32, 256, 2, 2, HD).transpose(0, 1, 3, 2, 4).reshape(32, 1024, HD)
-    dr = jnp.concatenate([decay[0], rate[0]], axis=0).T
-    dr = jnp.broadcast_to(dr[:, :, None], (2, 16, HD))
     hbm = pl.BlockSpec(memory_space=pl.ANY)
     vmem = pl.BlockSpec(memory_space=pltpu.VMEM)
+    smem = pl.BlockSpec(memory_space=pltpu.SMEM)
     V = pltpu.VMEM
     dma = pltpu.SemaphoreType.DMA
     mixed, new_state = pl.pallas_call(
@@ -513,7 +527,7 @@
             jax.ShapeDtypeStruct((512, 256), BF16),
             jax.ShapeDtypeStruct((2, HD, HD), F32),
         ),
-        in_specs=[hbm, vmem, hbm, hbm, hbm, pl.BlockSpec(memory_space=pltpu.SMEM), hbm, hbm],
+        in_specs=[hbm, vmem, hbm, hbm, hbm, smem, hbm, smem, smem],
         out_specs=(vmem, vmem),
         scratch_shapes=[
             V((2, 512, 1024), BF16),
@@ -521,9 +535,10 @@
             V((5, 1024, HD), BF16),
             V((32, 1024, HD), BF16),
             V((1024, HD), F32),
+            V((32, 256, HD), BF16), V((32, VR, 256), BF16),
+            V((32, 256, HD), BF16), V((32, VR, 256), BF16),
             V((32, 256, HD), BF16), V((32, HD, 256), BF16),
-            V((32, 256, HD), BF16), V((32, HD, 256), BF16),
-            V((32, 256, HD), BF16), V((32, HD, 256), BF16),
+            V((32, 2, 256, HD), F32),
             V((2, 16, 2, HD, 256), BF16),
             V((2, 16, 2, HD, 256), BF16),
             V((2, 16, 2, 2, 256), F32),
@@ -534,11 +549,11 @@
             V((2, 2, HD, 256), F32), V((2, 2, HD, 256), F32), V((2, 512, HD), F32),
             V((2, 2, HD, 256), F32),
             V((2, HD, HD), F32), V((2, HD, HD), F32),
-            V((2, 16, HD), F32), V((2, NP, HD), BF16),
+            V((2, 16, HD), F32), V((2, 16, HD), F32), V((2, NP, HD), BF16),
             V((2, 2, HD, 256), BF16), V((2, 8, HD, 256), BF16),
             V((8, 256, HD), BF16),
             V((3, HD, HD), F32),
-            dma((9,)), dma((4,)), dma((4,)), dma((2, 4)), dma((2, 4)), dma((4, 2)), dma((4, 2)),
+            dma((9,)), dma((4,)), dma((4,)), dma((3, 4)), dma((3, 4)), dma((4, 2)), dma((4, 2)),
             dma((2, 16, 4)), dma((2, 16, 2)), dma((2, 5, 4, 2)), dma((2, 5, 4, 2)),
             dma((7,)), dma((4, 2)), dma((2, 7)), dma((2, 4, 2)),
         ],
@@ -546,7 +561,7 @@
             collective_id=0, has_side_effects=True, vmem_limit_bytes=60 * 1024 * 1024
         ),
         name="prefill",
-    )(tokens, norm_gain[None], w_attn, persist_kv, kv, cache_len, mem_state[0], dr)
+    )(tokens, norm_gain[None], w_attn, persist_kv, kv, cache_len, mem_state[0], decay[0].T, rate[0].T)
     return (mixed, new_state[None])
 
 

time: 110 us -> 92.2 us (0.84)
  Pallas kernels: 105 us -> 88.1 us
    pallas_call x1, Pallas kernels: 105 us -> 88.1 us  [shards(): pl.pallas_call(kernel, out_shape=(jax.ShapeDtypeStruct((512, 256), BF16),...]
where the time goes in v2:
time: 92.2 us; the launch traced here: 92 us
  Pallas kernels  88.1 us (96%)
  local copies, waits for them, and re-layouts  3.24 us (4%)
    pallas_call x1, Pallas kernels, shards(): pl.pallas_call(kernel, out_shape=(jax.ShapeDtypeStruct((512, 256), BF16),...  88.1 us
    unnamed x2, local copies, waits for them, and re-layouts  3.24 us

profile of v2, /device:TPU:1, one launch (start us, length us, event | category | flops | bytes accessed | tf_op | source)
XLA Modules:
  0.0 92.0 jit_solution(2812378841341935875)
XLA Ops:
  0.6 88.1 %prefill.1 = (bf16[512,256]{1,0:T(8,128)(2,1)}, f32[2,128,128]{2,1,0:T(8,128)}) custom-call(bf16[512,1024]{1,0:T(8,128)(2,1)} %tok_hbm.1, f32[1,1024]{1,0:T(1,128)} %bitcast.17, bf16[5,256,256]{2,1,0:T(8,128)(2,1)} %w_hbm.1, bf16[2,16,256]{2,1,0:T(8,128)(2,1)} %persist_hbm.1, bf16[32,1024,128]{2,1,0:T(8,128)(2,1)} %bitcast.14, s32[32]{0:T(128)} %clen_ref.1, ...), custom_call_target="tpu_custom_call" | custom-call | tf_op jit(solution)/shard_map/prefill/pallas_call | solution.py:524
  88.8 1.7 %copy.14 = bf16[512,256]{1,0:T(8,128)(2,1)} copy(bf16[512,256]{1,0:T(8,128)(2,1)} %get-tuple-element.8) | data formatting | bytes 524288
  90.4 1.6 %copy.15 = f32[1,2,128,128]{3,2,1,0:T(8,128)} copy(f32[1,2,128,128]{3,2,1,0:T(8,128)} %bitcast.16) | data formatting | bytes 262144
